TPU v7x, 256 devices: a whole 4x4x8 slice. The times are simulated.
256 devices in a mesh: dp: 64 (over z, y, core), section: 4 (over x).
Axes of the slice: x: 4, y: 4, z: 8, core: 2. Of those that a mesh axis runs over, the one named last changes fastest.
Arguments:
- query_hidden: bfloat16 [32768, 4096], P('dp', 'section'), may hold values from -0.5 to 0.5
- tool_hidden: bfloat16 [32768, 4096], P('dp', 'section'), may hold values from -0.5 to 0.5
- norm_gain: float32 [4096], P('section'), may hold values from 0.5 to 1.5
- positive_tool: int32 [32768], P('dp'), may hold values from 0 to 511
- hard_owner: int32 [32768, 2], P('dp'), may hold values from 0 to 63, as said below
- hard_row: int32 [32768, 2], P('dp'), may hold values from 0 to 511
- hard_valid: int32 [32768, 2], P('dp'), may hold values from 0 to 1
Outputs:
- query_grad: bfloat16 [32768, 4096], P('dp', 'section')
- tool_grad: bfloat16 [32768, 4096], P('dp', 'section')
- gain_grad: float32 [4096], P('section')
Inputs may be any that keep to these rules, and one draw needn't show every extreme that they name: `hard_owner`: each dp index's valid slots name any one owner at most 32 times; two owners, the same for every dp index and drawn from the seed, are named exactly 32 times by the valid slots of every dp index.
All inputs are finite; a program needn't handle non-finite values.
Results may differ from a plain program's by a relative error of at most 0.0067.
Values may be sent and summed in bfloat16 or wider, within the bound.
A program may use at most 128 MiB of HBM per device.

v0:
```python
import jax
import jax.numpy as jnp
import numpy as np
from jax import lax
from jax.sharding import Mesh
from jax.sharding import PartitionSpec as P

EPSILON = 1e-06
SOFTMAX_TEMP = 0.05
DP = ("dz", "dy", "dc")


def softmax_grads(shard_scores, negative_scores, positive, valid_mask):
    selected_rows = lax.broadcasted_iota(jnp.int32, shard_scores.shape, 1) == positive[:, None]
    softmax_weights = jnp.exp(shard_scores / SOFTMAX_TEMP)
    shard_probabilities = softmax_weights / jnp.sum(softmax_weights, axis=1, keepdims=True)
    positive_score = jnp.sum(jnp.where(selected_rows, shard_scores, 0.0), axis=1)
    positive_weight = jnp.exp(positive_score / SOFTMAX_TEMP)
    negative_weights = jnp.where(valid_mask > 0, jnp.exp(negative_scores / SOFTMAX_TEMP), 0.0)
    negative_weight_sum = positive_weight + jnp.sum(negative_weights, axis=1)
    shard_gradients = (
        (
            shard_probabilities
            + jnp.where(selected_rows, (positive_weight / negative_weight_sum - 2.0)[:, None], 0.0)
        )
        / SOFTMAX_TEMP
    ).astype(jnp.bfloat16)
    negative_gradients = (negative_weights / (negative_weight_sum[:, None] * SOFTMAX_TEMP)).astype(
        jnp.bfloat16
    )
    return (shard_gradients, negative_gradients)


def body(query_hidden, tool_hidden, norm_gain, positive_tool, hard_owner, hard_row, hard_valid):
    query_count, features = query_hidden.shape
    tool_count = tool_hidden.shape[0]
    per_query = hard_owner.shape[1]
    slots = query_count * per_query
    group_size = lax.axis_size(DP)
    capacity = max(2, 2 * query_count * per_query // group_size)
    places = group_size * capacity
    owners = hard_owner.reshape(-1)
    wanted_rows = hard_row.reshape(-1)
    usable = hard_valid.reshape(-1) > 0
    slot_ids = jnp.arange(slots, dtype=jnp.int32)
    same_earlier = (
        (owners[:, None] == owners[None, :])
        & usable[None, :]
        & (slot_ids[None, :] < slot_ids[:, None])
    )
    slot_place = jnp.sum(same_earlier.astype(jnp.int32), axis=1)
    target = jnp.where(usable, owners * capacity + slot_place, places)
    place_ids = jnp.arange(places, dtype=jnp.int32)
    slot_at = target[:, None] == place_ids[None, :]
    requests = jnp.sum(jnp.where(slot_at, wanted_rows[:, None], 0), axis=0).reshape(
        group_size, capacity
    )
    indices = lax.all_to_all(requests, DP, 0, 0, tiled=True).reshape(-1)
    query_scaled = query_hidden.astype(jnp.float32) * norm_gain
    tool_scaled = tool_hidden.astype(jnp.float32) * norm_gain
    query_squares, tool_squares = lax.psum(
        (jnp.sum(query_scaled * query_scaled, axis=1), jnp.sum(tool_scaled * tool_scaled, axis=1)),
        "section",
    )
    query_norm = jnp.sqrt(query_squares + EPSILON)
    tool_norm = jnp.sqrt(tool_squares + EPSILON)
    query_unit32 = query_scaled / query_norm[:, None]
    tool_unit32 = tool_scaled / tool_norm[:, None]
    query_unit = query_unit32.astype(jnp.bfloat16)
    tool_unit = tool_unit32.astype(jnp.bfloat16)
    pick_tool = (indices[:, None] == jnp.arange(tool_count, dtype=jnp.int32)[None, :]).astype(
        jnp.bfloat16
    )
    answers = jnp.dot(pick_tool, tool_unit, preferred_element_type=jnp.float32).astype(jnp.bfloat16)
    slot_of_query = slot_at.reshape(query_count, per_query, places).any(axis=1)
    pick_query = slot_of_query.T.astype(jnp.bfloat16)
    sent_queries = jnp.dot(pick_query, query_unit, preferred_element_type=jnp.float32).astype(
        jnp.bfloat16
    )
    payload = jnp.concatenate(
        [
            answers.reshape(group_size, capacity, features),
            sent_queries.reshape(group_size, capacity, features),
        ],
        axis=1,
    )
    received = lax.all_to_all(payload, DP, 0, 0, tiled=True)
    back = received[:, :capacity].reshape(places, features)
    arrived = received[:, capacity:].reshape(places, features)
    local_part = lax.dot_general(
        query_unit, tool_unit, (((1,), (1,)), ((), ())), preferred_element_type=jnp.float32
    )
    hard_units = jnp.dot(
        slot_at.astype(jnp.bfloat16), back, preferred_element_type=jnp.float32
    ).reshape(query_count, per_query, features)
    hard_part = jnp.einsum(
        "qd,qkd->qk", query_unit.astype(jnp.float32), hard_units, preferred_element_type=jnp.float32
    )
    shard_scores, negative_scores = (
        lax.psum(local_part.astype(jnp.bfloat16), "section").astype(jnp.float32),
        lax.psum(hard_part.astype(jnp.bfloat16), "section").astype(jnp.float32),
    )
    shard_gradients, negative_gradients = softmax_grads(
        shard_scores, negative_scores, positive_tool, hard_valid
    )
    query_pull = jnp.dot(shard_gradients, tool_unit, preferred_element_type=jnp.float32)
    query_pull = query_pull + jnp.einsum(
        "qk,qkd->qd",
        negative_gradients.astype(jnp.float32),
        hard_units,
        preferred_element_type=jnp.float32,
    )
    sent_grads = jnp.sum(
        jnp.where(slot_at, negative_gradients.reshape(-1)[:, None].astype(jnp.float32), 0.0), axis=0
    ).astype(jnp.bfloat16)
    arrived_grads = lax.all_to_all(
        sent_grads.reshape(group_size, capacity), DP, 0, 0, tiled=True
    ).reshape(-1)
    weights = jnp.where(
        jnp.arange(tool_count, dtype=jnp.int32)[:, None] == indices[None, :],
        arrived_grads[None, :],
        0.0,
    ).astype(jnp.bfloat16)
    tool_pull = lax.dot_general(
        shard_gradients, query_unit, (((0,), (0,)), ((), ())), preferred_element_type=jnp.float32
    )
    tool_pull = tool_pull + jnp.dot(weights, arrived, preferred_element_type=jnp.float32)
    query_inner, tool_inner = lax.psum(
        (jnp.sum(query_unit32 * query_pull, axis=1), jnp.sum(tool_unit32 * tool_pull, axis=1)),
        "section",
    )
    query_back = (query_pull - query_unit32 * query_inner[:, None]) / query_norm[:, None]
    tool_back = (tool_pull - tool_unit32 * tool_inner[:, None]) / tool_norm[:, None]
    query_grad = (query_back * norm_gain).astype(jnp.bfloat16)
    tool_grad = (tool_back * norm_gain).astype(jnp.bfloat16)
    gain_terms = jnp.sum(query_back * query_hidden.astype(jnp.float32), axis=0) + jnp.sum(
        tool_back * tool_hidden.astype(jnp.float32), axis=0
    )
    gain_grad = lax.psum(lax.psum(lax.psum(gain_terms, "dc"), "dy"), "dz")
    return (query_grad, tool_grad, gain_grad)


def split_dp(mesh):
    dp = mesh.shape["dp"]
    cores = 2 if dp % 2 == 0 else 1
    rest = dp // cores
    ys = 4 if rest % 4 == 0 else 1
    devices = np.asarray(mesh.devices).reshape(rest // ys, ys, cores, mesh.shape["section"])
    return Mesh(devices, DP + ("section",))


def solution(mesh):
    fine = split_dp(mesh)
    return jax.shard_map(
        body,
        mesh=fine,
        in_specs=(
            P(DP, "section"),
            P(DP, "section"),
            P("section"),
            P(DP),
            P(DP, None),
            P(DP, None),
            P(DP, None),
        ),
        out_specs=(P(DP, "section"), P(DP, "section"), P("section")),
        check_vma=False,
    )
```

profile of v0, /device:TPU:2, one launch (start us, length us, event | category | flops | bytes accessed | tf_op | source)
XLA Modules:
  0.0 356.6 jit_solution(10480050438670012715)
XLA Ops:
  7.2 0.0 copy-start.7
  7.2 0.0 copy-start.6
  7.2 0.0 copy-start
  7.2 0.9 copy.34
  8.1 0.2 eq.95
  8.3 0.7 broadcast_compare_fusion
  9.0 0.2 copy.35
  9.2 0.2 gt.22
  9.4 0.6 convert_reduce_fusion
  10.0 0.8 copy.37
  10.8 0.0 copy-start.5
  10.8 0.2 broadcast_in_dim.88
  11.0 1.1 select_reduce_fusion.1
  12.1 0.7 all_to_all.13
  12.8 12.1 %all-to-all-start = ((s32[64,1,32]{2,1,0:T(1,128)}), s32[64,1,32]{2,1,0:T(1,128)S(1)}, u32[]{:S(2)}, u32[]{:S(2)}) async-start(s32[64,1,32]{2,1,0:T(1,128)} %bitcast.2), calls=%async_computation | async-start | bytes 65536 | tf_op jit(solution)/shard_map/all_to_all | solution.py:58
  24.9 0.2 reduce_sum.115
  25.1 0.0 copy-done
  25.2 1.8 fusion.17
  27.0 8.6 %all-reduce.1 = (f32[512]{0:T(512)S(1)}, f32[512]{0:T(512)S(1)}) all-reduce(f32[512]{0:T(512)S(1)} %get-tuple-element.8, f32[512]{0:T(512)S(1)} %get-tuple-element.7), channel_id=1, replica_groups=mesh['dz'=8,'dy'=4,'dc'=2,'section'=4] {'section'}, use_global_device_ids=true, to_apply=%region_1.2 | all-reduce | flops 1024 | bytes 8192 | tf_op jit(solution)/shard_map/psum | solution.py:61
  35.6 0.1 copy.36
  35.7 0.0 copy-done.7
  35.8 1.1 fusion.3
  36.9 0.0 copy-start.1
  36.9 4.5 %convolution_convert_fusion = bf16[2048,1024]{1,0:T(8,128)(2,1)} fusion(pred[512,2048]{1,0:T(8,128)(4,1)S(1)} %fusion.3, f32[512]{0:T(512)S(1)} %add_sqrt_fusion.1, f32[1024]{0:T(1024)S(1)} %copy-done.5, bf16[512,1024]{1,0:T(8,128)(2,1)S(1)} %copy-done), kind=kOutput, calls=%fused_computation.18 | convolution fusion | flops 2151677952 | bytes 6297600 | tf_op jit(solution)/shard_map/dot_general | solution.py:77
  41.4 0.0 all-to-all-done
  41.4 0.5 broadcast.95
  41.9 0.7 reduce.4
  42.7 0.1 eq.106
  42.7 4.2 %fusion.8 = bf16[2048,1024]{1,0:T(8,128)(2,1)} fusion(s32[2048]{0:T(1024)S(1)} %eq.106, bf16[512,1024]{1,0:T(8,128)(2,1)S(1)} %copy-done.1, f32[512]{0:T(512)S(1)} %add_sqrt_fusion, f32[1024]{0:T(1024)S(1)} %copy-done.5), kind=kOutput, calls=%fused_computation.17 | convolution fusion | flops 2152726528 | bytes 5257216 | tf_op jit(solution)/shard_map/dot_general | solution.py:74
  46.9 8.5 %pad_maximum_fusion = bf16[64,64,1024]{2,1,0:T(8,128)(2,1)} fusion(bf16[64,32,1024]{2,1,0:T(8,128)(2,1)} %bitcast.23, bf16[64,32,1024]{2,1,0:T(8,128)(2,1)} %bitcast.25), kind=kLoop, calls=%fused_computation | loop fusion | flops 16777216 | bytes 16777216 | tf_op jit(solution)/shard_map/concatenate | solution.py:80
  55.4 10.6 %all-to-all-start.1 = ((bf16[64,64,1024]{2,1,0:T(8,128)(2,1)}), bf16[64,64,1024]{2,1,0:T(8,128)(2,1)}, u32[]{:S(2)}, u32[]{:S(2)}) async-start(bf16[64,64,1024]{2,1,0:T(8,128)(2,1)} %pad_maximum_fusion), calls=%async_computation.1 | async-start | bytes 16777216 | tf_op jit(solution)/shard_map/all_to_all | solution.py:87
  66.0 0.2 all-reduce.4.cloned.1.call-start
  66.2 1.6 convolution_convert_fusion.1
  67.9 0.0 all-reduce.4.cloned.1.call-update
  67.9 0.3 fusion.47
  68.2 49.4 %all-reduce.4.cloned.1.call-done = bf16[512,512]{1,0:T(8,128)(2,1)} async-done(((bf16[512,512]{1,0:T(8,128)(2,1)}), bf16[512,512]{1,0:T(8,128)(2,1)}) %all-reduce.4.cloned.1.call-update) | async-done | bytes 524304 | tf_op jit(solution)/shard_map/psum | solution.py:100
  117.6 1.5 fusion.28
  119.1 133.1 %all-to-all-done.1 = bf16[64,64,1024]{2,1,0:T(8,128)(2,1)} async-done(((bf16[64,64,1024]{2,1,0:T(8,128)(2,1)}), bf16[64,64,1024]{2,1,0:T(8,128)(2,1)}, u32[]{:S(2)}, u32[]{:S(2)}) %all-to-all-start.1) | async-done | bytes 8388640 | tf_op jit(solution)/shard_map/all_to_all | solution.py:87
  252.2 5.4 %fusion.50 = (bf16[64,32,1024]{2,1,0:T(8,128)(2,1)}, bf16[64,32,1024]{2,1,0:T(8,128)(2,1)S(1)}) fusion(bf16[64,64,1024]{2,1,0:T(8,128)(2,1)} %all-to-all-done.1), kind=kLoop, calls=%fused_computation.78 | loop fusion | bytes 16777216 | tf_op jit(solution)/shard_map/slice | solution.py:89
  257.5 4.8 %fusion.1 = bf16[512,2,1024]{2,0,1:T(8,128)(2,1)S(1)} fusion(bf16[2048,1024,1]{1,0,2:T(8,128)(2,1)S(1)} %bitcast.24, s32[512,2]{0,1:T(2,128)S(1)} %add_select_fusion.1), kind=kOutput, calls=%fused_computation.7 | convolution fusion | flops 4297064448 | bytes 6295552 | tf_op jit(solution)/shard_map/dot_general | solution.py:93
  262.4 1.3 copy-done.9
  263.7 8.8 %fusion.11 = bf16[512,1,2]{2,1,0:T(2,128)(2,1)S(1)} fusion(bf16[512,2,1024]{2,0,1:T(8,128)(2,1)S(1)} %fusion.1, bf16[512,1024,1]{1,0,2:T(8,128)(2,1)S(1)} %fusion.47), kind=kOutput, calls=%fused_computation.21 | convolution fusion | flops 2097152 | bytes 3147776 | tf_op jit(solution)/shard_map/qd,qkd->qk/dot_general | solution.py:96
  272.6 0.1 copy.43
  272.7 10.1 %psum.66 = bf16[512,2]{0,1:T(2,128)(2,1)S(1)} all-reduce(bf16[512,2]{0,1:T(2,128)(2,1)S(1)} %bitcast.27), channel_id=1, replica_groups=mesh['dz'=8,'dy'=4,'dc'=2,'section'=4] {'section'}, use_global_device_ids=true, to_apply=%region_10.11 | all-reduce | flops 1024 | bytes 4096 | tf_op jit(solution)/shard_map/psum | solution.py:101
  282.9 0.2 copy.39
  283.0 0.2 reshape.138
  283.2 1.2 select_reduce_fusion
  284.4 0.7 convert_element_type.99
  285.1 6.4 %all-to-all-start.2 = ((bf16[64,1,32]{2,1,0:T(2,128)(2,1)}), bf16[64,1,32]{2,1,0:T(2,128)(2,1)S(1)}, u32[]{:S(2)}, u32[]{:S(2)}) async-start(bf16[64,1,32]{2,1,0:T(2,128)(2,1)} %convert_element_type.99), calls=%async_computation.2 | async-start | bytes 65536 | tf_op jit(solution)/shard_map/all_to_all | solution.py:116
  291.5 0.2 copy.44
  291.8 4.1 %fusion.9 = f32[512,1,1024]{2,1,0:T(1,128)S(1)} fusion(bf16[512,2,1]{1,2,0:T(2,128)(2,1)S(1)} %copy.44, bf16[512,2,1024]{2,0,1:T(8,128)(2,1)} %copy-done.9), kind=kOutput, calls=%fused_computation.19 | convolution fusion | flops 2097152 | bytes 4196352 | tf_op jit(solution)/shard_map/qk,qkd->qd/dot_general | solution.py:107
  295.9 2.5 bitcast_add_fusion
  298.4 2.5 all-to-all-done.2
  300.9 0.1 reduce.1
  301.0 0.1 broadcast_in_dim.95
  301.1 4.7 %fusion.21 = f32[512,1024]{1,0:T(8,128)S(1)} fusion(bf16[2048,1024]{1,0:T(8,128)(2,1)} %bitcast.22, s32[2048]{0:T(1024)S(1)} %eq.106, bf16[2048]{0:T(1024)(128)(2,1)S(1)} %broadcast_in_dim.95), kind=kOutput, calls=%fused_computation.35 | convolution fusion | flops 2149580800 | bytes 6303744 | tf_op jit(solution)/shard_map/dot_general | solution.py:127
  305.7 2.9 multiply_reduce_fusion
  308.7 7.7 %all-reduce = (f32[512]{0:T(512)S(1)}, f32[512]{0:T(512)S(1)}) all-reduce(f32[512]{0:T(512)S(1)} %get-tuple-element.6, f32[512]{0:T(512)S(1)} %get-tuple-element.5), channel_id=1, replica_groups=mesh['dz'=8,'dy'=4,'dc'=2,'section'=4] {'section'}, use_global_device_ids=true, to_apply=%region_13.14 | all-reduce | flops 1024 | bytes 8192 | tf_op jit(solution)/shard_map/psum | solution.py:128
  316.4 2.4 fusion.20
  318.8 1.9 fusion.19
  320.6 2.4 psum.69
  323.1 8.8 %psum.70 = f32[1024]{0:T(1024)S(1)} all-reduce(f32[1024]{0:T(1024)S(1)} %psum.69), channel_id=1, replica_groups=mesh['dz'=8,'dy'=4,'dc'=2,'section'=4] {'dy'}, use_global_device_ids=true, to_apply=%region_20.21 | all-reduce | flops 1024 | bytes 8192 | tf_op jit(solution)/shard_map/psum | solution.py:139
  331.8 16.7 %psum.71 = f32[1024]{0:T(1024)} all-reduce(f32[1024]{0:T(1024)S(1)} %psum.70), channel_id=1, replica_groups=mesh['dz'=8,'dy'=4,'dc'=2,'section'=4] {'dz'}, use_global_device_ids=true, to_apply=%region_21.22 | all-reduce | flops 1024 | bytes 8192 | tf_op jit(solution)/shard_map/psum | solution.py:139
  348.5 1.2 multiply_convert_fusion.1
  (20 shorter events, 0.1 us)
Async XLA Ops:
  7.2 28.6 %copy-start.7 = (s32[512,2]{0,1:T(2,128)S(1)}, s32[512,2]{0,1:T(2,128)}, u32[]{:S(2)}) copy-start(s32[512,2]{0,1:T(2,128)} %param.11) | copy-start | bytes 12292
  7.2 28.6 %copy-start.6 = (s32[512,2]{0,1:T(2,128)S(1)}, s32[512,2]{0,1:T(2,128)}, u32[]{:S(2)}) copy-start(s32[512,2]{0,1:T(2,128)} %param.13) | copy-start | bytes 12292
  7.2 18.0 %copy-start = (bf16[512,1024]{1,0:T(8,128)(2,1)S(1)}, bf16[512,1024]{1,0:T(8,128)(2,1)}, u32[]{:S(2)}) copy-start(bf16[512,1024]{1,0:T(8,128)(2,1)} %param.7) | copy-start | bytes 3145732
  10.8 26.1 %copy-start.5 = (f32[1024]{0:T(1024)S(1)}, f32[1024]{0:T(1024)}, u32[]{:S(2)}) copy-start(f32[1024]{0:T(1024)} %param.9) | copy-start | bytes 12292
  12.8 28.6 %all-to-all-start = ((s32[64,1,32]{2,1,0:T(1,128)}), s32[64,1,32]{2,1,0:T(1,128)S(1)}, u32[]{:S(2)}, u32[]{:S(2)}) async-start(s32[64,1,32]{2,1,0:T(1,128)} %bitcast.2), calls=%async_computation | async-start | bytes 65536 | tf_op jit(solution)/shard_map/all_to_all | solution.py:58
  36.9 5.8 %copy-start.1 = (bf16[512,1024]{1,0:T(8,128)(2,1)S(1)}, bf16[512,1024]{1,0:T(8,128)(2,1)}, u32[]{:S(2)}) copy-start(bf16[512,1024]{1,0:T(8,128)(2,1)} %param.8) | copy-start | bytes 3145732
  55.4 196.7 %all-to-all-start.1 = ((bf16[64,64,1024]{2,1,0:T(8,128)(2,1)}), bf16[64,64,1024]{2,1,0:T(8,128)(2,1)}, u32[]{:S(2)}, u32[]{:S(2)}) async-start(bf16[64,64,1024]{2,1,0:T(8,128)(2,1)} %pad_maximum_fusion), calls=%async_computation.1 | async-start | bytes 16777216 | tf_op jit(solution)/shard_map/all_to_all | solution.py:87
  66.0 51.6 %all-reduce.4.cloned.1.call-start = ((), (), s32[]{:S(2)}) async-start(), calls=%async_computation.3 | async-start | bytes 1048576 | tf_op jit(solution)/shard_map/psum | solution.py:100
  67.9 49.7 %copy-start.8 = (s32[512]{0:T(512)S(1)}, s32[512]{0:T(512)}, u32[]{:S(2)}) copy-start(s32[512]{0:T(512)} %param.10) | copy-start | bytes 6148
  262.4 1.3 copy-start.9
  285.1 15.7 %all-to-all-start.2 = ((bf16[64,1,32]{2,1,0:T(2,128)(2,1)}), bf16[64,1,32]{2,1,0:T(2,128)(2,1)S(1)}, u32[]{:S(2)}, u32[]{:S(2)}) async-start(bf16[64,1,32]{2,1,0:T(2,128)(2,1)} %convert_element_type.99), calls=%async_computation.2 | async-start | bytes 65536 | tf_op jit(solution)/shard_map/all_to_all | solution.py:116
  291.7 4.1 %copy-start.4 = (bf16[512,512]{1,0:T(8,128)(2,1)S(1)}, bf16[512,512]{1,0:T(8,128)(2,1)}, u32[]{:S(2)}) copy-start(bf16[512,512]{1,0:T(8,128)(2,1)} %all-reduce.4.cloned.1.call-done) | copy-start | bytes 1572868
  301.1 4.7 %copy-start.2 = (f32[512,1024]{1,0:T(8,128)S(1)}, f32[512,1024]{1,0:T(8,128)}, u32[]{:S(2)}) copy-start(f32[512,1024]{1,0:T(8,128)} %bitcast_add_fusion) | copy-start | bytes 6291460
  316.4 2.4 copy-start.3
Sparse Core Ops, SparseCore 0:
  69.7 47.8 all-reduce.3
where the time goes:
time: 357 us
  waiting for transfers between devices  185 us (52%)
  blocking collectives  54.3 us (15%)
  matrix products  38.2 us (11%)
  starting transfers between devices  29.3 us (8%)
  other arithmetic  23.3 us (7%)
  between operations  14.3 us (4%)
  local copies, waits for them, and re-layouts  12.2 us (3%)
    all_to_all x1, waiting for transfers between devices, body(): received = lax.all_to_all(payload, DP, 0, 0, tiled=True)  133 us
    psum x1, waiting for transfers between devices, body(): lax.psum(local_part.astype(jnp.bfloat16), 'section').astype(jnp.float32)  49.4 us
    psum x3, blocking collectives, body(): gain_grad = lax.psum(lax.psum(lax.psum(gain_terms, 'dc'), 'dy'), 'dz')  27.9 us
    all_to_all x1, starting transfers between devices, body(): indices = lax.all_to_all(requests, DP, 0, 0, tiled=True).reshape(-1)  12.1 us
    all_to_all x1, starting transfers between devices, body(): received = lax.all_to_all(payload, DP, 0, 0, tiled=True)  10.6 us
    psum x1, blocking collectives, body(): lax.psum(hard_part.astype(jnp.bfloat16), 'section').astype(jnp.float32)  10.1 us
    dot_general x1, matrix products, body(): jnp.einsum('qd,qkd->qk', query_unit.astype(jnp.float32), hard_units, pref...  8.83 us
    psum x1, blocking collectives, body(): lax.psum((jnp.sum(query_scaled * query_scaled, axis=1), jnp.sum(tool_scal...  8.62 us
  transfers between devices with their start and end apart: 4, of which 3 were waited for; matrix products, arithmetic and copies ran while one was open for 5% of the time, Pallas kernels for 0%

commit v1 on v0

--- a/solution.py
+++ b/solution.py
@@ -98,7 +98,9 @@
     )
     shard_scores, negative_scores = (
         lax.psum(local_part.astype(jnp.bfloat16), "section").astype(jnp.float32),
-        lax.psum(hard_part.astype(jnp.bfloat16), "section").astype(jnp.float32),
+        jnp.sum(lax.all_gather(hard_part.astype(jnp.bfloat16), "section"), axis=0).astype(
+            jnp.float32
+        ),
     )
     shard_gradients, negative_gradients = softmax_grads(
         shard_scores, negative_scores, positive_tool, hard_valid

time: 357 us -> 360 us (level)
    all_gather x0 -> x1, blocking collectives: none -> 10.9 us  [body(): lax.all_gather(hard_part.astype(jnp.bfloat16), 'section')]
    psum x1 -> x0, blocking collectives: 10.1 us -> none  [body(): lax.psum(hard_part.astype(jnp.bfloat16), 'section').astype(jnp.float32)]
where the time goes in v1:
time: 360 us; the launch traced here: 359 us
  waiting for transfers between devices  185 us (51%)
  blocking collectives  57.1 us (16%)
  matrix products  38.2 us (11%)
  starting transfers between devices  29.2 us (8%)
  other arithmetic  23.3 us (6%)
  between operations  14.3 us (4%)
  local copies, waits for them, and re-layouts  12.2 us (3%)
    all_to_all x1, waiting for transfers between devices, body(): received = lax.all_to_all(payload, DP, 0, 0, tiled=True)  133 us
    psum x1, waiting for transfers between devices, body(): lax.psum(local_part.astype(jnp.bfloat16), 'section').astype(jnp.float32)  49.4 us
    psum x3, blocking collectives, body(): gain_grad = lax.psum(lax.psum(lax.psum(gain_terms, 'dc'), 'dy'), 'dz')  27.9 us
    all_to_all x1, starting transfers between devices, body(): indices = lax.all_to_all(requests, DP, 0, 0, tiled=True).reshape(-1)  12.1 us
    all_gather x1, blocking collectives, body(): lax.all_gather(hard_part.astype(jnp.bfloat16), 'section')  10.9 us
    all_to_all x1, starting transfers between devices, body(): received = lax.all_to_all(payload, DP, 0, 0, tiled=True)  10.6 us
    psum x1, blocking collectives, body(): lax.psum((jnp.sum(query_unit32 * query_pull, axis=1), jnp.sum(tool_unit32...  9.65 us
    dot_general x1, matrix products, body(): jnp.einsum('qd,qkd->qk', query_unit.astype(jnp.float32), hard_units, pref...  8.83 us
  transfers between devices with their start and end apart: 4, of which 3 were waited for; matrix products, arithmetic and copies ran while one was open for 5% of the time, Pallas kernels for 0%

profile of v1, /device:TPU:2, one launch (start us, length us, event | category | flops | bytes accessed | tf_op | source)
XLA Modules:
  0.0 359.4 jit_solution(1573743411470300359)
XLA Ops:
  7.2 0.0 copy-start.7
  7.2 0.0 copy-start.6
  7.2 0.0 copy-start
  7.2 0.9 copy.25
  8.1 0.2 eq.95
  8.3 0.7 broadcast_compare_fusion
  9.0 0.2 copy.26
  9.2 0.2 gt.22
  9.4 0.6 convert_reduce_fusion
  10.0 0.8 copy.28
  10.8 0.0 copy-start.5
  10.8 0.2 broadcast_in_dim.88
  11.0 1.1 select_reduce_fusion.1
  12.1 0.7 all_to_all.13
  12.8 12.1 %all-to-all-start = ((s32[64,1,32]{2,1,0:T(1,128)}), s32[64,1,32]{2,1,0:T(1,128)S(1)}, u32[]{:S(2)}, u32[]{:S(2)}) async-start(s32[64,1,32]{2,1,0:T(1,128)} %bitcast.2), calls=%async_computation | async-start | bytes 65536 | tf_op jit(solution)/shard_map/all_to_all | solution.py:58
  24.9 0.2 reduce_sum.127
  25.1 0.0 copy-done
  25.2 1.8 fusion.17
  27.0 8.6 %all-reduce.1 = (f32[512]{0:T(512)S(1)}, f32[512]{0:T(512)S(1)}) all-reduce(f32[512]{0:T(512)S(1)} %get-tuple-element.8, f32[512]{0:T(512)S(1)} %get-tuple-element.7), channel_id=1, replica_groups=mesh['dz'=8,'dy'=4,'dc'=2,'section'=4] {'section'}, use_global_device_ids=true, to_apply=%region_1.2 | all-reduce | flops 1024 | bytes 8192 | tf_op jit(solution)/shard_map/psum | solution.py:61
  35.6 0.1 copy.27
  35.8 1.1 fusion.3
  36.9 0.0 copy-start.1
  36.9 4.5 %convolution_convert_fusion = bf16[2048,1024]{1,0:T(8,128)(2,1)} fusion(pred[512,2048]{1,0:T(8,128)(4,1)S(1)} %fusion.3, f32[512]{0:T(512)S(1)} %add_sqrt_fusion.1, f32[1024]{0:T(1024)S(1)} %copy-done.5, bf16[512,1024]{1,0:T(8,128)(2,1)S(1)} %copy-done), kind=kOutput, calls=%fused_computation.18 | convolution fusion | flops 2151677952 | bytes 6297600 | tf_op jit(solution)/shard_map/dot_general | solution.py:77
  41.4 0.0 all-to-all-done
  41.4 0.5 broadcast.95
  41.9 0.7 reduce.5
  42.7 0.1 eq.106
  42.7 4.2 %fusion.8 = bf16[2048,1024]{1,0:T(8,128)(2,1)} fusion(s32[2048]{0:T(1024)S(1)} %eq.106, bf16[512,1024]{1,0:T(8,128)(2,1)S(1)} %copy-done.1, f32[512]{0:T(512)S(1)} %add_sqrt_fusion, f32[1024]{0:T(1024)S(1)} %copy-done.5), kind=kOutput, calls=%fused_computation.17 | convolution fusion | flops 2152726528 | bytes 5257216 | tf_op jit(solution)/shard_map/dot_general | solution.py:74
  46.9 8.5 %pad_maximum_fusion = bf16[64,64,1024]{2,1,0:T(8,128)(2,1)} fusion(bf16[64,32,1024]{2,1,0:T(8,128)(2,1)} %bitcast.25, bf16[64,32,1024]{2,1,0:T(8,128)(2,1)} %bitcast.27), kind=kLoop, calls=%fused_computation | loop fusion | flops 16777216 | bytes 16777216 | tf_op jit(solution)/shard_map/concatenate | solution.py:80
  55.4 10.6 %all-to-all-start.1 = ((bf16[64,64,1024]{2,1,0:T(8,128)(2,1)}), bf16[64,64,1024]{2,1,0:T(8,128)(2,1)}, u32[]{:S(2)}, u32[]{:S(2)}) async-start(bf16[64,64,1024]{2,1,0:T(8,128)(2,1)} %pad_maximum_fusion), calls=%async_computation.1 | async-start | bytes 16777216 | tf_op jit(solution)/shard_map/all_to_all | solution.py:87
  66.0 0.2 all-reduce.4.cloned.1.call-start
  66.2 1.6 convolution_convert_fusion.1
  67.9 0.0 all-reduce.4.cloned.1.call-update
  67.9 0.3 fusion.47
  68.2 49.4 %all-reduce.4.cloned.1.call-done = bf16[512,512]{1,0:T(8,128)(2,1)} async-done(((bf16[512,512]{1,0:T(8,128)(2,1)}), bf16[512,512]{1,0:T(8,128)(2,1)}) %all-reduce.4.cloned.1.call-update) | async-done | bytes 524304 | tf_op jit(solution)/shard_map/psum | solution.py:100
  117.6 1.5 fusion.28
  119.1 133.1 %all-to-all-done.1 = bf16[64,64,1024]{2,1,0:T(8,128)(2,1)} async-done(((bf16[64,64,1024]{2,1,0:T(8,128)(2,1)}), bf16[64,64,1024]{2,1,0:T(8,128)(2,1)}, u32[]{:S(2)}, u32[]{:S(2)}) %all-to-all-start.1) | async-done | bytes 8388640 | tf_op jit(solution)/shard_map/all_to_all | solution.py:87
  252.2 5.4 %fusion.50 = (bf16[64,32,1024]{2,1,0:T(8,128)(2,1)}, bf16[64,32,1024]{2,1,0:T(8,128)(2,1)S(1)}) fusion(bf16[64,64,1024]{2,1,0:T(8,128)(2,1)} %all-to-all-done.1), kind=kLoop, calls=%fused_computation.78 | loop fusion | bytes 16777216 | tf_op jit(solution)/shard_map/slice | solution.py:89
  257.5 4.8 %fusion.1 = bf16[512,2,1024]{2,0,1:T(8,128)(2,1)S(1)} fusion(bf16[2048,1024,1]{1,0,2:T(8,128)(2,1)S(1)} %bitcast.26, s32[512,2]{0,1:T(2,128)S(1)} %add_select_fusion.1), kind=kOutput, calls=%fused_computation.7 | convolution fusion | flops 4297064448 | bytes 6295552 | tf_op jit(solution)/shard_map/dot_general | solution.py:93
  262.4 1.3 copy-done.9
  263.7 8.8 %fusion.11 = bf16[512,1,2]{2,1,0:T(2,128)(2,1)S(1)} fusion(bf16[512,2,1024]{2,0,1:T(8,128)(2,1)S(1)} %fusion.1, bf16[512,1024,1]{1,0,2:T(8,128)(2,1)S(1)} %fusion.47), kind=kOutput, calls=%fused_computation.21 | convolution fusion | flops 2097152 | bytes 3147776 | tf_op jit(solution)/shard_map/qd,qkd->qk/dot_general | solution.py:96
  272.6 0.1 copy.34
  272.7 10.9 %all-gather = bf16[2048,2]{0,1:T(2,128)(2,1)S(1)} all-gather(bf16[512,2]{0,1:T(2,128)(2,1)S(1)} %bitcast.29), channel_id=2, replica_groups=mesh['dz'=8,'dy'=4,'dc'=2,'section'=4] {'section'}, dimensions={0}, use_global_device_ids=true | all-gather | bytes 10240 | tf_op jit(solution)/shard_map/all_gather | solution.py:101
  283.7 0.2 copy.30
  283.9 0.2 reshape.138
  284.0 1.2 select_reduce_fusion
  285.3 0.7 convert_element_type.101
  286.0 6.3 %all-to-all-start.2 = ((bf16[64,1,32]{2,1,0:T(2,128)(2,1)}), bf16[64,1,32]{2,1,0:T(2,128)(2,1)S(1)}, u32[]{:S(2)}, u32[]{:S(2)}) async-start(bf16[64,1,32]{2,1,0:T(2,128)(2,1)} %convert_element_type.101), calls=%async_computation.2 | async-start | bytes 65536 | tf_op jit(solution)/shard_map/all_to_all | solution.py:118
  292.3 0.2 copy.35
  292.5 0.0 copy-start.4
  292.5 4.1 %fusion.9 = f32[512,1,1024]{2,1,0:T(1,128)S(1)} fusion(bf16[512,2,1]{1,2,0:T(2,128)(2,1)S(1)} %copy.35, bf16[512,2,1024]{2,0,1:T(8,128)(2,1)} %copy-done.9), kind=kOutput, calls=%fused_computation.19 | convolution fusion | flops 2097152 | bytes 4196352 | tf_op jit(solution)/shard_map/qk,qkd->qd/dot_general | solution.py:109
  296.6 2.5 bitcast_add_fusion
  299.1 2.5 all-to-all-done.2
  301.6 0.1 reduce.2
  301.7 0.1 broadcast_in_dim.95
  301.8 4.7 %fusion.21 = f32[512,1024]{1,0:T(8,128)S(1)} fusion(bf16[2048,1024]{1,0:T(8,128)(2,1)} %bitcast.24, s32[2048]{0:T(1024)S(1)} %eq.106, bf16[2048]{0:T(1024)(128)(2,1)S(1)} %broadcast_in_dim.95), kind=kOutput, calls=%fused_computation.35 | convolution fusion | flops 2149580800 | bytes 6303744 | tf_op jit(solution)/shard_map/dot_general | solution.py:129
  306.5 2.9 multiply_reduce_fusion
  309.5 9.7 %all-reduce = (f32[512]{0:T(512)S(1)}, f32[512]{0:T(512)S(1)}) all-reduce(f32[512]{0:T(512)S(1)} %get-tuple-element.6, f32[512]{0:T(512)S(1)} %get-tuple-element.5), channel_id=1, replica_groups=mesh['dz'=8,'dy'=4,'dc'=2,'section'=4] {'section'}, use_global_device_ids=true, to_apply=%region_13.14 | all-reduce | flops 1024 | bytes 8192 | tf_op jit(solution)/shard_map/psum | solution.py:130
  319.1 2.4 fusion.20
  321.5 1.9 fusion.19
  323.4 2.4 psum.61
  325.8 8.8 %psum.62 = f32[1024]{0:T(1024)S(1)} all-reduce(f32[1024]{0:T(1024)S(1)} %psum.61), channel_id=1, replica_groups=mesh['dz'=8,'dy'=4,'dc'=2,'section'=4] {'dy'}, use_global_device_ids=true, to_apply=%region_20.21 | all-reduce | flops 1024 | bytes 8192 | tf_op jit(solution)/shard_map/psum | solution.py:141
  334.6 16.7 %psum.63 = f32[1024]{0:T(1024)} all-reduce(f32[1024]{0:T(1024)S(1)} %psum.62), channel_id=1, replica_groups=mesh['dz'=8,'dy'=4,'dc'=2,'section'=4] {'dz'}, use_global_device_ids=true, to_apply=%region_21.22 | all-reduce | flops 1024 | bytes 8192 | tf_op jit(solution)/shard_map/psum | solution.py:141
  351.3 1.2 multiply_convert_fusion.1
  (22 shorter events, 0.2 us)
Async XLA Ops:
  7.2 28.6 %copy-start.7 = (s32[512,2]{0,1:T(2,128)S(1)}, s32[512,2]{0,1:T(2,128)}, u32[]{:S(2)}) copy-start(s32[512,2]{0,1:T(2,128)} %param.11) | copy-start | bytes 12292
  7.2 28.6 %copy-start.6 = (s32[512,2]{0,1:T(2,128)S(1)}, s32[512,2]{0,1:T(2,128)}, u32[]{:S(2)}) copy-start(s32[512,2]{0,1:T(2,128)} %param.13) | copy-start | bytes 12292
  7.2 18.0 %copy-start = (bf16[512,1024]{1,0:T(8,128)(2,1)S(1)}, bf16[512,1024]{1,0:T(8,128)(2,1)}, u32[]{:S(2)}) copy-start(bf16[512,1024]{1,0:T(8,128)(2,1)} %param.7) | copy-start | bytes 3145732
  10.8 26.1 %copy-start.5 = (f32[1024]{0:T(1024)S(1)}, f32[1024]{0:T(1024)}, u32[]{:S(2)}) copy-start(f32[1024]{0:T(1024)} %param.9) | copy-start | bytes 12292
  12.8 28.6 %all-to-all-start = ((s32[64,1,32]{2,1,0:T(1,128)}), s32[64,1,32]{2,1,0:T(1,128)S(1)}, u32[]{:S(2)}, u32[]{:S(2)}) async-start(s32[64,1,32]{2,1,0:T(1,128)} %bitcast.2), calls=%async_computation | async-start | bytes 65536 | tf_op jit(solution)/shard_map/all_to_all | solution.py:58
  36.9 5.8 %copy-start.1 = (bf16[512,1024]{1,0:T(8,128)(2,1)S(1)}, bf16[512,1024]{1,0:T(8,128)(2,1)}, u32[]{:S(2)}) copy-start(bf16[512,1024]{1,0:T(8,128)(2,1)} %param.8) | copy-start | bytes 3145732
  55.4 196.7 %all-to-all-start.1 = ((bf16[64,64,1024]{2,1,0:T(8,128)(2,1)}), bf16[64,64,1024]{2,1,0:T(8,128)(2,1)}, u32[]{:S(2)}, u32[]{:S(2)}) async-start(bf16[64,64,1024]{2,1,0:T(8,128)(2,1)} %pad_maximum_fusion), calls=%async_computation.1 | async-start | bytes 16777216 | tf_op jit(solution)/shard_map/all_to_all | solution.py:87
  66.0 51.6 %all-reduce.4.cloned.1.call-start = ((), (), s32[]{:S(2)}) async-start(), calls=%async_computation.3 | async-start | bytes 1048576 | tf_op jit(solution)/shard_map/psum | solution.py:100
  67.9 49.7 %copy-start.8 = (s32[512]{0:T(512)S(1)}, s32[512]{0:T(512)}, u32[]{:S(2)}) copy-start(s32[512]{0:T(512)} %param.10) | copy-start | bytes 6148
  262.4 1.3 copy-start.9
  286.0 15.7 %all-to-all-start.2 = ((bf16[64,1,32]{2,1,0:T(2,128)(2,1)}), bf16[64,1,32]{2,1,0:T(2,128)(2,1)S(1)}, u32[]{:S(2)}, u32[]{:S(2)}) async-start(bf16[64,1,32]{2,1,0:T(2,128)(2,1)} %convert_element_type.101), calls=%async_computation.2 | async-start | bytes 65536 | tf_op jit(solution)/shard_map/all_to_all | solution.py:118
  292.5 4.1 %copy-start.4 = (bf16[512,512]{1,0:T(8,128)(2,1)S(1)}, bf16[512,512]{1,0:T(8,128)(2,1)}, u32[]{:S(2)}) copy-start(bf16[512,512]{1,0:T(8,128)(2,1)} %all-reduce.4.cloned.1.call-done) | copy-start | bytes 1572868
  301.8 4.7 %copy-start.2 = (f32[512,1024]{1,0:T(8,128)S(1)}, f32[512,1024]{1,0:T(8,128)}, u32[]{:S(2)}) copy-start(f32[512,1024]{1,0:T(8,128)} %bitcast_add_fusion) | copy-start | bytes 6291460
  319.1 2.4 copy-start.3
Sparse Core Ops, SparseCore 0:
  69.7 47.8 all-reduce.3
